TPU v7x, 128 devices: a whole 4x4x4 slice. The times are simulated.
128 devices in a mesh: row: 8 (over y, z_hi), col: 16 (over x, z_lo, core).
Axes of the slice: x: 4, y: 4, z: 4 (z_hi: 2, z_lo: 2; z = z_hi * 2 + z_lo), core: 2. Of those that a mesh axis runs over, the one named last changes fastest.
Arguments:
- voltages: bfloat16 [2, 64, 64, 2, 31744], P(None, 'row', 'col'), may hold values from -6 to 6
- fir: float32 [16, 1024], replicated, may hold values from -0.046875 to 0.046875
Outputs:
- power: float32 [64, 64, 2, 1024], P('col', None, None, 'row')
All inputs are finite; a program needn't handle non-finite values.
Results may differ from a plain program's by a relative error of at most 0.0032.
Values may be sent and summed in bfloat16 or wider, within the bound.
No kernel may reach another device: no remote copies, remote signals or barrier semaphores. Data moves between devices by JAX's collectives and lax.ppermute only.
A program may use at most 192 MiB of HBM per device.

v0:
```python
import functools

import jax
import jax.numpy as jnp
import numpy as np
from jax import lax
from jax.experimental import pallas as pl
from jax.experimental.pallas import tpu as pltpu
from jax.sharding import PartitionSpec as P

NROW = 64
NCOL = 64
POL = 2
NCHAN = 1024
TAPS = 16
FRAMES = 16
ROWS = 8
COLS = 16
A = NROW // ROWS
B = NCOL // COLS
BLOCKS = FRAMES + TAPS - 1
LANES = 128
F32 = jnp.float32
BF16 = jnp.bfloat16


def bf16_pair(angle):
    cosine = np.cos(angle).astype(np.float32).astype(jnp.bfloat16)
    sine = np.sin(angle).astype(np.float32).astype(jnp.bfloat16)
    return cosine, sine


def complex_table(angle):
    cosine, sine = bf16_pair(angle)
    real = np.stack([cosine, sine], axis=-1)
    imag = np.stack([-sine, cosine], axis=-1)
    return np.stack([real, imag], axis=1)


def dft_table():
    k = np.arange(256)
    table = complex_table(2.0 * np.pi * (np.outer(k, k) % 256) / 256)
    return table.transpose(0, 1, 3, 2).reshape(512, 512)


def twiddle_table():
    n = np.arange(256)
    angle = 2.0 * np.pi * np.outer(np.arange(4), n) / NCHAN
    return np.concatenate([np.cos(angle), np.sin(angle)]).astype(np.float32)


def spatial(length):
    index = np.arange(length)
    return complex_table(2.0 * np.pi * (np.outer(index, index) % length) / length)


def row_matrix():
    table = spatial(NROW).reshape(NROW, 2, ROWS, A, 2)
    return table.transpose(0, 1, 2, 4, 3).reshape(2 * NROW, 2 * NROW)


def col_matrix():
    return spatial(NCOL).transpose(1, 0, 3, 2).reshape(2 * NCOL, 2 * NCOL)


def sum_matrix():
    eye = np.eye(8, dtype=np.float32).reshape(2, 4, 2, 4)
    full = np.einsum("hqHQ,pP,f->phqHQPf", eye, np.eye(2, dtype=np.float32), np.ones(FRAMES, np.float32))
    return (full.reshape(16, 256) / (FRAMES * NROW * NCOL)).astype(jnp.bfloat16)


def channelize_kernel(x_ref, fir_ref, dft_ref, tw_ref, out_ref, coef, filt, zed, turn):
    @pl.when(pl.program_id(0) == 0)
    def _():
        for s in range(8):
            piece = fir_ref[:, s * LANES:(s + 1) * LANES]
            for p in range(POL):
                coef[pl.ds(2 * s + p, TAPS, stride=16), :] = piece

    def filter_one(unit, carry):
        half = unit % 2
        part = (unit // 2) % 2
        which = unit // 4
        ant = 2 * carry + which
        taps = [coef[pl.ds(pl.multiple_of(16 * t + 8 * half, 8), 8), :] for t in range(TAPS)]
        xs = [
            x_ref[part, ant, 0, pl.ds(pl.multiple_of(16 * i + 8 * half, 8), 8), :].astype(F32)
            for i in range(BLOCKS)
        ]
        for f in range(FRAMES):
            terms = [taps[t] * xs[f + t] for t in range(TAPS)]
            while len(terms) > 1:
                terms = [a + b for a, b in zip(terms[::2], terms[1::2])]
            filt[which, part, pl.ds(pl.multiple_of(16 * f + 8 * half, 8), 8), :] = terms[0]
        return carry

    def pair_step(pair, carry):
        lax.fori_loop(0, 8, filter_one, pair)
        for which in range(2):
            for p in range(POL):
                for lo in range(2):
                    re = []
                    im = []
                    for j in range(4):
                        row = 2 * (2 * j + lo) + p
                        re.append(filt[which, 0, pl.ds(row, FRAMES, stride=16), :])
                        im.append(filt[which, 1, pl.ds(row, FRAMES, stride=16), :])
                    sr0, si0 = re[0] + re[2], im[0] + im[2]
                    sr1, si1 = re[1] + re[3], im[1] + im[3]
                    dr0, di0 = re[0] - re[2], im[0] - im[2]
                    dr1, di1 = re[1] - re[3], im[1] - im[3]
                    outs = [
                        (sr0 + sr1, si0 + si1),
                        (dr0 + di1, di0 - dr1),
                        (sr0 - sr1, si0 - si1),
                        (dr0 - di1, di0 + dr1),
                    ]
                    for q in range(4):
                        zr, zi = outs[q]
                        if q > 0:
                            cosine = tw_ref[q:q + 1, lo * LANES:(lo + 1) * LANES]
                            sine = tw_ref[4 + q:5 + q, lo * LANES:(lo + 1) * LANES]
                            zr, zi = zr * cosine + zi * sine, zi * cosine - zr * sine
                        r0 = which * LANES + q * 32 + p * 16
                        zed[r0:r0 + 16, lo * LANES:(lo + 1) * LANES] = zr.astype(BF16)
                        zed[r0:r0 + 16, (2 + lo) * LANES:(3 + lo) * LANES] = zi.astype(BF16)
        spec = lax.dot_general(
            dft_ref[...], zed[...], (((1,), (1,)), ((), ())), preferred_element_type=F32
        )
        for which in range(2):
            turn[pl.ds(2 * pair + which, 512, stride=A), :] = spec[:, which * LANES:(which + 1) * LANES]
        return carry

    lax.fori_loop(0, A // 2, pair_step, 0)
    out_ref[:, 0] = turn[...].reshape(128, 2, 16, LANES).astype(BF16)


def channelize(volts, fir):
    flat = volts.reshape(2, A, B, POL, BLOCKS * 8, LANES)
    flat = flat.swapaxes(3, 4).reshape(2, A, B, BLOCKS * 16, LANES)
    return pl.pallas_call(
        channelize_kernel,
        name="channelize",
        grid=(B,),
        in_specs=[
            pl.BlockSpec((2, A, 1, BLOCKS * 16, LANES), lambda b: (0, 0, b, 0, 0)),
            pl.BlockSpec((TAPS, NCHAN), lambda b: (0, 0)),
            pl.BlockSpec((512, 512), lambda b: (0, 0)),
            pl.BlockSpec((8, 256), lambda b: (0, 0)),
        ],
        out_specs=pl.BlockSpec((128, 1, 2, 16, LANES), lambda b: (0, b, 0, 0, 0)),
        out_shape=jax.ShapeDtypeStruct((128, B, 2, 16, LANES), BF16),
        scratch_shapes=[
            pltpu.VMEM((TAPS * 16, LANES), F32),
            pltpu.VMEM((2, 2, FRAMES * 16, LANES), F32),
            pltpu.VMEM((256, 512), BF16),
            pltpu.VMEM((512 * A, LANES), F32),
        ],
        compiler_params=pltpu.CompilerParams(vmem_limit_bytes=40 << 20),
    )(flat, fir, jnp.asarray(dft_table()), jnp.asarray(twiddle_table()))


def beam_kernel(in_ref, row_ref, col_ref, sum_ref, out_ref, turn):
    step = pl.program_id(0)

    def row_step(i, carry):
        b4 = i % B
        col = i // B
        b = i
        for h in range(2):
            piece = in_ref[:, col, b4, h].reshape(128, LANES)
            got = jnp.dot(row_ref[...], piece, preferred_element_type=F32)
            turn[h, pl.ds(b, 128, stride=NCOL), :] = got
        return carry

    lax.fori_loop(0, NCOL, row_step, 0)

    def col_step(g, carry):
        pows = []
        for j in range(4):
            base = pl.multiple_of((4 * g + j) * 128, 128)
            halves = []
            for h in range(2):
                mid = turn[h, pl.ds(base, 128), :].astype(BF16)
                beam = jnp.dot(col_ref[...], mid, preferred_element_type=F32)
                re = beam[:NCOL]
                im = beam[NCOL:]
                halves.append((re * re + im * im).astype(BF16))
            pows.append(jnp.concatenate(halves, axis=1))
        power = jnp.concatenate(pows, axis=0)
        out_ref[g] = lax.dot_general(
            sum_ref[...], power, (((1,), (1,)), ((), ())), preferred_element_type=F32
        )
        return carry

    lax.fori_loop(0, COLS, col_step, 0)


def beamform(got):
    return pl.pallas_call(
        beam_kernel,
        name="beamform",
        grid=(1,),
        in_specs=[
            pl.BlockSpec((ROWS, COLS, B, 2, 16, LANES), lambda i: (0, 0, 0, 0, 0, 0)),
            pl.BlockSpec((128, 128), lambda i: (0, 0)),
            pl.BlockSpec((128, 128), lambda i: (0, 0)),
            pl.BlockSpec((16, 256), lambda i: (0, 0)),
        ],
        out_specs=pl.BlockSpec((COLS, 16, 256), lambda i: (0, 0, 0)),
        out_shape=jax.ShapeDtypeStruct((COLS, 16, 256), F32),
        scratch_shapes=[pltpu.VMEM((2, 128 * NCOL, LANES), F32)],
        compiler_params=pltpu.CompilerParams(vmem_limit_bytes=40 << 20),
    )(
        got.reshape(ROWS, COLS, B, 2, 16, LANES),
        jnp.asarray(row_matrix()),
        jnp.asarray(col_matrix()),
        jnp.asarray(sum_matrix()),
    )


def finish_kernel(in_ref, out_ref):
    for p in range(POL):
        piece = in_ref[:, p * 8:(p + 1) * 8, :].reshape(128, 256)
        out_ref[pl.ds(p, 256, stride=2), :] = piece.T


def finish(got):
    return pl.pallas_call(
        finish_kernel,
        name="finish",
        out_shape=jax.ShapeDtypeStruct((256 * POL, LANES), F32),
    )(got)


def body(volts, fir):
    spectra = channelize(volts, fir)
    gathered = lax.all_to_all(spectra, ("row", "col"), 0, 0, tiled=True)
    partial = beamform(gathered)
    swapped = lax.all_to_all(partial, "col", 0, 0, tiled=True)
    return finish(swapped).reshape(NROW // COLS, NCOL, POL, LANES)


def solution(mesh):
    in_specs = (P(None, "row", "col", None, None), P())
    out_specs = P("col", None, None, "row")
    return jax.shard_map(body, mesh=mesh, in_specs=in_specs, out_specs=out_specs, check_vma=False)
```

profile of v0, /device:TPU:1, one launch (start us, length us, event | category | flops | bytes accessed | tf_op | source)
XLA Modules:
  0.0 129.2 jit_solution(12272855696351654000)
XLA Ops:
  0.0 0.0 copy-start
  0.0 3.3 %copy-done = bf16[2,8,4,2,31744]{4,3,2,1,0:T(2,128)(2,1)S(1)} copy-done((bf16[2,8,4,2,31744]{4,3,2,1,0:T(2,128)(2,1)S(1)}, bf16[2,8,4,2,31744]{4,3,2,1,0:T(2,128)(2,1)}, u32[]{:S(2)}) %copy-start) | copy-done | bytes 8126488
  3.3 0.0 copy-start.1
  3.3 1.0 copy-done.1
  4.3 0.0 copy-start.2
  4.4 0.8 copy-done.2
  5.2 0.0 copy-start.6
  5.2 0.7 copy-done.6
  5.9 21.6 %channelize.1 = bf16[128,4,2,16,128]{4,3,2,1,0:T(8,128)(2,1)S(1)} custom-call(bf16[2,8,4,496,128]{4,3,2,1,0:T(8,128)(2,1)S(1)} %bitcast.8, f32[16,1024]{1,0:T(8,128)S(1)} %copy-done.2, bf16[512,512]{1,0:T(8,128)(2,1)S(1)} %copy-done.1, f32[8,256]{1,0:T(8,128)S(1)} %copy-done.6), custom_call_target="tpu_custom_call" | custom-call | tf_op jit(solution)/shard_map/channelize/pallas_call | solution.py:141
  27.5 0.0 copy-start.3
  27.5 0.0 copy-start.4
  27.5 0.0 copy-start.5
  27.5 63.7 %all_to_all.10 = bf16[128,4,2,16,128]{4,3,2,1,0:T(8,128)(2,1)S(1)} all-to-all(bf16[128,4,2,16,128]{4,3,2,1,0:T(8,128)(2,1)S(1)} %channelize.1), channel_id=1, replica_groups=mesh['row'=8,'col'=16] {'row','col'}, dimensions={0} | all-to-all | bytes 8388608 | tf_op jit(solution)/shard_map/all_to_all | solution.py:238
  91.2 0.0 copy-done.3
  91.2 0.0 copy-done.4
  91.2 0.0 copy-done.5
  91.2 23.3 %beamform.1 = f32[16,16,256]{2,1,0:T(8,128)S(1)} custom-call(bf16[8,16,4,2,16,128]{5,4,3,2,1,0:T(8,128)(2,1)S(1)} %bitcast.7, bf16[128,128]{1,0:T(8,128)(2,1)S(1)} %copy-done.4, bf16[128,128]{1,0:T(8,128)(2,1)S(1)} %copy-done.3, bf16[16,256]{1,0:T(8,128)(2,1)S(1)} %copy-done.5), custom_call_target="tpu_custom_call" | custom-call | tf_op jit(solution)/shard_map/beamform/pallas_call | solution.py:200
  114.5 12.9 %all_to_all.11.in_ref = f32[16,16,256]{2,1,0:T(8,128)} all-to-all(f32[16,16,256]{2,1,0:T(8,128)S(1)} %beamform.1), channel_id=1, replica_groups=mesh['row'=8,'col'=16] {'col'}, dimensions={0} | all-to-all | bytes 524288 | tf_op jit(solution)/shard_map/all_to_all | solution.py:240
  127.4 1.8 %finish.1 = f32[512,128]{1,0:T(8,128)} custom-call(f32[16,16,256]{2,1,0:T(8,128)} %all_to_all.11.in_ref), custom_call_target="tpu_custom_call" | custom-call | tf_op jit(solution)/shard_map/finish/pallas_call | solution.py:229
Async XLA Ops:
  0.0 3.3 %copy-start = (bf16[2,8,4,2,31744]{4,3,2,1,0:T(2,128)(2,1)S(1)}, bf16[2,8,4,2,31744]{4,3,2,1,0:T(2,128)(2,1)}, u32[]{:S(2)}) copy-start(bf16[2,8,4,2,31744]{4,3,2,1,0:T(2,128)(2,1)} %param.7) | copy-start | bytes 24379396
  3.3 1.0 copy-start.1
  4.3 0.8 copy-start.2
  5.2 0.7 copy-start.6
  27.5 63.7 %copy-start.3 = (bf16[128,128]{1,0:T(8,128)(2,1)S(1)}, bf16[128,128]{1,0:T(8,128)(2,1)}, u32[]{:S(2)}) copy-start(bf16[128,128]{1,0:T(8,128)(2,1)} %constant.13.clone.col_ref) | copy-start | bytes 98308
  27.5 63.7 %copy-start.4 = (bf16[128,128]{1,0:T(8,128)(2,1)S(1)}, bf16[128,128]{1,0:T(8,128)(2,1)}, u32[]{:S(2)}) copy-start(bf16[128,128]{1,0:T(8,128)(2,1)} %constant.12.clone.row_ref) | copy-start | bytes 98308
  27.5 63.7 %copy-start.5 = (bf16[16,256]{1,0:T(8,128)(2,1)S(1)}, bf16[16,256]{1,0:T(8,128)(2,1)}, u32[]{:S(2)}) copy-start(bf16[16,256]{1,0:T(8,128)(2,1)} %constant.14.clone.sum_ref) | copy-start | bytes 24580
where the time goes:
time: 130 us; the launch traced here: 129 us
  blocking collectives  76.6 us (59%)
  Pallas kernels  46.7 us (36%)
  local copies, waits for them, and re-layouts  5.9 us (5%)
    all_to_all x1, blocking collectives, body(): gathered = lax.all_to_all(spectra, ('row', 'col'), 0, 0, tiled=True)  63.7 us
    pallas_call x1, Pallas kernels, beamform(): pl.pallas_call(beam_kernel, name='beamform', grid=(1,), in_specs=[pl.Bloc...  23.3 us
    pallas_call x1, Pallas kernels, channelize(): pl.pallas_call(channelize_kernel, name='channelize', grid=(B,), in_specs=...  21.6 us
    all_to_all x1, blocking collectives, body(): swapped = lax.all_to_all(partial, 'col', 0, 0, tiled=True)  12.9 us
    unnamed x14, local copies, waits for them, and re-layouts  5.9 us

commit v1 on v0

v1 whole, which is shorter than its diff:
```python
import functools

import jax
import jax.numpy as jnp
import numpy as np
from jax import lax
from jax.experimental import pallas as pl
from jax.experimental.pallas import tpu as pltpu
from jax.sharding import PartitionSpec as P

NROW = 64
NCOL = 64
POL = 2
NCHAN = 1024
TAPS = 16
FRAMES = 16
ROWS = 8
COLS = 16
A = NROW // ROWS
B = NCOL // COLS
BLOCKS = FRAMES + TAPS - 1
LANES = 128
GROUP = 4
F32 = jnp.float32
BF16 = jnp.bfloat16


def bf16_pair(angle):
    cosine = np.cos(angle).astype(np.float32).astype(jnp.bfloat16)
    sine = np.sin(angle).astype(np.float32).astype(jnp.bfloat16)
    return cosine, sine


def complex_table(angle):
    cosine, sine = bf16_pair(angle)
    real = np.stack([cosine, sine], axis=-1)
    imag = np.stack([-sine, cosine], axis=-1)
    return np.stack([real, imag], axis=1)


def dft_table():
    k = np.arange(256)
    table = complex_table(2.0 * np.pi * (np.outer(k, k) % 256) / 256)
    return table.transpose(0, 1, 3, 2).reshape(512, 512)


def twiddle_table():
    n = np.arange(256)
    angle = 2.0 * np.pi * np.outer(np.arange(4), n) / NCHAN
    return np.concatenate([np.cos(angle), np.sin(angle)]).astype(np.float32)


def spatial(length):
    index = np.arange(length)
    return complex_table(2.0 * np.pi * (np.outer(index, index) % length) / length)


def row_matrix():
    table = spatial(NROW).reshape(NROW, 2, ROWS, A, 2)
    return table.transpose(0, 1, 2, 4, 3).reshape(2 * NROW, 2 * NROW)


def col_matrix():
    table = spatial(NCOL).reshape(NCOL, 2, 8, 8, 2)
    return table.transpose(1, 0, 2, 4, 3).reshape(2 * NCOL, 2 * NCOL)


def sum_matrix():
    eye = np.eye(8, dtype=np.float32).reshape(2, 4, 2, 4)
    full = np.einsum("hqHQ,pP,f->phqHQPf", eye, np.eye(2, dtype=np.float32), np.ones(FRAMES, np.float32))
    return (full.reshape(16, 256) / (FRAMES * NROW * NCOL)).astype(jnp.bfloat16)


def channelize_kernel(x_hbm, fir_hbm, dft_hbm, tw_hbm, out_ref, x_ref, fir_ref, dft_ref, tw_ref, coef, filt, zed, turn, sems):
    x_copies = [pltpu.make_async_copy(x_hbm.at[:, :, b], x_ref.at[b], sems.at[b]) for b in range(B)]
    fir_copy = pltpu.make_async_copy(fir_hbm, fir_ref, sems.at[B])
    dft_copy = pltpu.make_async_copy(dft_hbm, dft_ref, sems.at[B + 1])
    tw_copy = pltpu.make_async_copy(tw_hbm, tw_ref, sems.at[B + 2])
    fir_copy.start()
    x_copies[0].start()
    tw_copy.start()
    dft_copy.start()
    for b in range(1, B):
        x_copies[b].start()
    fir_copy.wait()
    for s in range(8):
        piece = fir_ref[:, s * LANES:(s + 1) * LANES]
        for p in range(POL):
            coef[pl.ds(2 * s + p, TAPS, stride=16), :] = piece

    def filter_pair(index):
        col = index // (A // 2)
        pair = index % (A // 2)
        for which in range(2):
            for part in range(2):
                taps = [coef[16 * t:16 * t + 16, :].astype(BF16) for t in range(TAPS)]
                xs = [x_ref[col, part, 2 * pair + which, 16 * i:16 * i + 16, :] for i in range(BLOCKS)]
                for f in range(FRAMES):
                    terms = [taps[t] * xs[f + t] for t in range(TAPS)]
                    while len(terms) > TAPS // GROUP:
                        terms = [a + b for a, b in zip(terms[::2], terms[1::2])]
                    terms = [t.astype(F32) for t in terms]
                    while len(terms) > 1:
                        terms = [a + b for a, b in zip(terms[::2], terms[1::2])]
                    row = (f // 8) * 128 + f % 8
                    filt[which, part, pl.ds(row, 16, stride=8), :] = terms[0]

    def load_rows(which, part, row):
        lo = filt[which, part, row * 8:row * 8 + 8, :]
        hi = filt[which, part, 128 + row * 8:128 + row * 8 + 8, :]
        return jnp.concatenate([lo, hi], axis=0)

    def butterfly():
        for which in range(2):
            for p in range(POL):
                for lo in range(2):
                    rows = [2 * (2 * j + lo) + p for j in range(4)]
                    re = [load_rows(which, 0, row) for row in rows]
                    im = [load_rows(which, 1, row) for row in rows]
                    sr0, si0 = re[0] + re[2], im[0] + im[2]
                    sr1, si1 = re[1] + re[3], im[1] + im[3]
                    dr0, di0 = re[0] - re[2], im[0] - im[2]
                    dr1, di1 = re[1] - re[3], im[1] - im[3]
                    outs = [
                        (sr0 + sr1, si0 + si1),
                        (dr0 + di1, di0 - dr1),
                        (sr0 - sr1, si0 - si1),
                        (dr0 - di1, di0 + dr1),
                    ]
                    for q in range(4):
                        zr, zi = outs[q]
                        if q > 0:
                            cosine = tw_ref[q:q + 1, lo * LANES:(lo + 1) * LANES]
                            sine = tw_ref[4 + q:5 + q, lo * LANES:(lo + 1) * LANES]
                            zr, zi = zr * cosine + zi * sine, zi * cosine - zr * sine
                        r0 = which * LANES + q * 32 + p * 16
                        zed[r0:r0 + 16, lo * LANES:(lo + 1) * LANES] = zr.astype(BF16)
                        zed[r0:r0 + 16, (2 + lo) * LANES:(3 + lo) * LANES] = zi.astype(BF16)

    x_copies[0].wait()
    filter_pair(0)
    tw_copy.wait()
    dft_copy.wait()

    def col_step(col, carry):
        @pl.when(col < B - 1)
        def _():
            pltpu.make_async_copy(x_hbm.at[:, :, col + 1], x_ref.at[col + 1], sems.at[col + 1]).wait()

        def pair_step(pair, carry):
            butterfly()
            filter_pair(jnp.minimum(col * (A // 2) + pair + 1, B * A // 2 - 1))
            spec = lax.dot_general(
                dft_ref[...], zed[...], (((1,), (1,)), ((), ())), preferred_element_type=F32
            )
            for which in range(2):
                turn[pl.ds(2 * pair + which, 512, stride=A), :] = spec[:, which * LANES:(which + 1) * LANES]
            return carry

        lax.fori_loop(0, A // 2, pair_step, 0)
        out_ref[:, col] = turn[...].reshape(128, 2, 16, LANES).astype(BF16)
        return carry

    lax.fori_loop(0, B, col_step, 0)


def in_hbm(x):
    return pltpu.with_memory_space_constraint(x, pltpu.HBM)


def channelize(volts, fir):
    flat = volts.reshape(2, A, B, POL, BLOCKS * 8, LANES)
    flat = flat.swapaxes(3, 4).reshape(2, A, B, BLOCKS * 16, LANES)
    return pl.pallas_call(
        channelize_kernel,
        name="channelize",
        in_specs=[pl.BlockSpec(memory_space=pltpu.HBM)] * 4,
        out_shape=jax.ShapeDtypeStruct((128, B, 2, 16, LANES), BF16),
        scratch_shapes=[
            pltpu.VMEM((B, 2, A, BLOCKS * 16, LANES), BF16),
            pltpu.VMEM((TAPS, NCHAN), F32),
            pltpu.VMEM((512, 512), BF16),
            pltpu.VMEM((8, 256), F32),
            pltpu.VMEM((TAPS * 16, LANES), F32),
            pltpu.VMEM((2, 2, FRAMES * 16, LANES), F32),
            pltpu.VMEM((256, 512), BF16),
            pltpu.VMEM((512 * A, LANES), F32),
            pltpu.SemaphoreType.DMA((B + 3,)),
        ],
        compiler_params=pltpu.CompilerParams(vmem_limit_bytes=40 << 20),
    )(in_hbm(flat), in_hbm(fir), in_hbm(jnp.asarray(dft_table())), in_hbm(jnp.asarray(twiddle_table())))


def beam_kernel(in_ref, row_ref, col_ref, sum_ref, out_ref, turn):
    def row_step(high, carry):
        for low in range(8):
            piece = jnp.concatenate(
                [in_ref[:, 2 * high + low // B, low % B, h].reshape(128, LANES) for h in range(2)], axis=1
            )
            got = jnp.dot(row_ref[...], piece, preferred_element_type=F32)
            for h in range(2):
                turn[h, pl.ds(high * 1024 + low, 128, stride=8), :] = got[:, h * LANES:(h + 1) * LANES]
        return carry

    lax.fori_loop(0, NCOL // 8, row_step, 0)

    def col_step(g, carry):
        pows = []
        for j in range(4):
            base = (4 * g + j) * 16
            mids = []
            for h in range(2):
                rows = [turn[h, pl.ds(pl.multiple_of(high * 1024 + base, 16), 16), :] for high in range(8)]
                mids.append(jnp.concatenate(rows, axis=0).astype(BF16))
            beam = jnp.dot(col_ref[...], jnp.concatenate(mids, axis=1), preferred_element_type=F32)
            re = beam[:NCOL]
            im = beam[NCOL:]
            pows.append((re * re + im * im).astype(BF16))
        power = jnp.concatenate(pows, axis=0)
        out_ref[g] = lax.dot_general(
            sum_ref[...], power, (((1,), (1,)), ((), ())), preferred_element_type=F32
        )
        return carry

    lax.fori_loop(0, COLS, col_step, 0)


def beamform(got):
    return pl.pallas_call(
        beam_kernel,
        name="beamform",
        out_shape=jax.ShapeDtypeStruct((COLS, 16, 256), F32),
        scratch_shapes=[pltpu.VMEM((2, 128 * NCOL, LANES), F32)],
        compiler_params=pltpu.CompilerParams(vmem_limit_bytes=40 << 20),
    )(
        got.reshape(ROWS, COLS, B, 2, 16, LANES),
        jnp.asarray(row_matrix()),
        jnp.asarray(col_matrix()),
        jnp.asarray(sum_matrix()),
    )


def finish_kernel(in_ref, out_ref):
    for p in range(POL):
        piece = in_ref[:, p * 8:(p + 1) * 8, :].reshape(128, 256)
        out_ref[pl.ds(p, 256, stride=2), :] = piece.T


def finish(got):
    return pl.pallas_call(
        finish_kernel,
        name="finish",
        out_shape=jax.ShapeDtypeStruct((256 * POL, LANES), F32),
    )(got)


def body(volts, fir):
    spectra = channelize(volts, fir)
    gathered = lax.all_to_all(spectra, ("row", "col"), 0, 0, tiled=True)
    partial = beamform(gathered)
    swapped = lax.all_to_all(partial, "col", 0, 0, tiled=True)
    return finish(swapped).reshape(NROW // COLS, NCOL, POL, LANES)


def solution(mesh):
    in_specs = (P(None, "row", "col", None, None), P())
    out_specs = P("col", None, None, "row")
    return jax.shard_map(body, mesh=mesh, in_specs=in_specs, out_specs=out_specs, check_vma=False)
```

time: 130 us -> 103 us (0.79)
  Pallas kernels: 46.7 us -> 25.8 us
  local copies, waits for them, and re-layouts: 5.9 us -> 0.02 us
    pallas_call x2, Pallas kernels: 44.9 us -> 24 us  [the longest x1 15.8 us: channelize(): pl.pallas_call(channelize_kernel, name='channelize', in_specs=[pl.BlockSp...]
    unnamed x14 -> x6, local copies, waits for them, and re-layouts: 5.9 us -> 0.02 us
where the time goes in v1:
time: 103 us; the launch traced here: 102 us
  blocking collectives  76.6 us (74%)
  Pallas kernels  25.8 us (25%)
    all_to_all x1, blocking collectives, body(): gathered = lax.all_to_all(spectra, ('row', 'col'), 0, 0, tiled=True)  63.7 us
    pallas_call x1, Pallas kernels, channelize(): pl.pallas_call(channelize_kernel, name='channelize', in_specs=[pl.BlockSp...  15.8 us
    all_to_all x1, blocking collectives, body(): swapped = lax.all_to_all(partial, 'col', 0, 0, tiled=True)  12.9 us
    pallas_call x1, Pallas kernels, beamform(): pl.pallas_call(beam_kernel, name='beamform', out_shape=jax.ShapeDtypeStru...  8.26 us

profile of v1, /device:TPU:1, one launch (start us, length us, event | category | flops | bytes accessed | tf_op | source)
XLA Modules:
  0.0 102.4 jit_solution(9234245769675752197)
XLA Ops:
  0.0 15.8 %channelize.1 = bf16[128,4,2,16,128]{4,3,2,1,0:T(8,128)(2,1)S(1)} custom-call(bf16[2,8,4,496,128]{4,3,2,1,0:T(8,128)(2,1)} %bitcast.8, f32[16,1024]{1,0:T(8,128)} %fir_hbm.1, bf16[512,512]{1,0:T(8,128)(2,1)} %constant.10.clone.dft_hbm, f32[8,256]{1,0:T(8,128)} %constant.11.clone.tw_hbm), custom_call_target="tpu_custom_call" | custom-call | tf_op jit(solution)/shard_map/channelize/pallas_call | solution.py:174
  15.8 0.0 copy-start
  15.8 0.0 copy-start.1
  15.8 0.0 copy-start.2
  15.8 63.7 %all_to_all.10 = bf16[128,4,2,16,128]{4,3,2,1,0:T(8,128)(2,1)S(1)} all-to-all(bf16[128,4,2,16,128]{4,3,2,1,0:T(8,128)(2,1)S(1)} %channelize.1), channel_id=1, replica_groups=mesh['row'=8,'col'=16] {'row','col'}, dimensions={0} | all-to-all | bytes 8388608 | tf_op jit(solution)/shard_map/all_to_all | solution.py:259
  79.5 0.0 copy-done
  79.5 0.0 copy-done.1
  79.5 0.0 copy-done.2
  79.5 8.3 %beamform.1 = f32[16,16,256]{2,1,0:T(8,128)S(1)} custom-call(bf16[8,16,4,2,16,128]{5,4,3,2,1,0:T(8,128)(2,1)S(1)} %bitcast.7, bf16[128,128]{1,0:T(8,128)(2,1)S(1)} %copy-done.1, bf16[128,128]{1,0:T(8,128)(2,1)S(1)} %copy-done, bf16[16,256]{1,0:T(8,128)(2,1)S(1)} %copy-done.2), custom_call_target="tpu_custom_call" | custom-call | tf_op jit(solution)/shard_map/beamform/pallas_call | solution.py:229
  87.7 12.9 %all_to_all.11.in_ref = f32[16,16,256]{2,1,0:T(8,128)} all-to-all(f32[16,16,256]{2,1,0:T(8,128)S(1)} %beamform.1), channel_id=1, replica_groups=mesh['row'=8,'col'=16] {'col'}, dimensions={0} | all-to-all | bytes 524288 | tf_op jit(solution)/shard_map/all_to_all | solution.py:261
  100.6 1.8 %finish.1 = f32[512,128]{1,0:T(8,128)} custom-call(f32[16,16,256]{2,1,0:T(8,128)} %all_to_all.11.in_ref), custom_call_target="tpu_custom_call" | custom-call | tf_op jit(solution)/shard_map/finish/pallas_call | solution.py:250
Async XLA Ops:
  15.8 63.7 %copy-start = (bf16[128,128]{1,0:T(8,128)(2,1)S(1)}, bf16[128,128]{1,0:T(8,128)(2,1)}, u32[]{:S(2)}) copy-start(bf16[128,128]{1,0:T(8,128)(2,1)} %constant.13.clone.col_ref) | copy-start | bytes 98308
  15.8 63.7 %copy-start.1 = (bf16[128,128]{1,0:T(8,128)(2,1)S(1)}, bf16[128,128]{1,0:T(8,128)(2,1)}, u32[]{:S(2)}) copy-start(bf16[128,128]{1,0:T(8,128)(2,1)} %constant.12.clone.row_ref) | copy-start | bytes 98308
  15.8 63.7 %copy-start.2 = (bf16[16,256]{1,0:T(8,128)(2,1)S(1)}, bf16[16,256]{1,0:T(8,128)(2,1)}, u32[]{:S(2)}) copy-start(bf16[16,256]{1,0:T(8,128)(2,1)} %constant.14.clone.sum_ref) | copy-start | bytes 24580

commit v2 on v1

--- a/solution.py
+++ b/solution.py
@@ -20,7 +20,7 @@
 B = NCOL // COLS
 BLOCKS = FRAMES + TAPS - 1
 LANES = 128
-GROUP = 4
+GROUP = 16
 F32 = jnp.float32
 BF16 = jnp.bfloat16
 
@@ -88,11 +88,10 @@
         for p in range(POL):
             coef[pl.ds(2 * s + p, TAPS, stride=16), :] = piece
 
-    def filter_pair(index):
+    def filter_pair(index, units=((0, 0), (0, 1), (1, 0), (1, 1))):
         col = index // (A // 2)
         pair = index % (A // 2)
-        for which in range(2):
-            for part in range(2):
+        for which, part in units:
                 taps = [coef[16 * t:16 * t + 16, :].astype(BF16) for t in range(TAPS)]
                 xs = [x_ref[col, part, 2 * pair + which, 16 * i:16 * i + 16, :] for i in range(BLOCKS)]
                 for f in range(FRAMES):
@@ -110,7 +109,7 @@
         hi = filt[which, part, 128 + row * 8:128 + row * 8 + 8, :]
         return jnp.concatenate([lo, hi], axis=0)
 
-    def butterfly():
+    def butterfly(slot):
         for which in range(2):
             for p in range(POL):
                 for lo in range(2):
@@ -134,8 +133,8 @@
                             sine = tw_ref[4 + q:5 + q, lo * LANES:(lo + 1) * LANES]
                             zr, zi = zr * cosine + zi * sine, zi * cosine - zr * sine
                         r0 = which * LANES + q * 32 + p * 16
-                        zed[r0:r0 + 16, lo * LANES:(lo + 1) * LANES] = zr.astype(BF16)
-                        zed[r0:r0 + 16, (2 + lo) * LANES:(3 + lo) * LANES] = zi.astype(BF16)
+                        zed[slot, r0:r0 + 16, lo * LANES:(lo + 1) * LANES] = zr.astype(BF16)
+                        zed[slot, r0:r0 + 16, (2 + lo) * LANES:(3 + lo) * LANES] = zi.astype(BF16)
 
     x_copies[0].wait()
     filter_pair(0)
@@ -148,20 +147,26 @@
             pltpu.make_async_copy(x_hbm.at[:, :, col + 1], x_ref.at[col + 1], sems.at[col + 1]).wait()
 
         def pair_step(pair, carry):
-            butterfly()
-            filter_pair(jnp.minimum(col * (A // 2) + pair + 1, B * A // 2 - 1))
+            index = col * (A // 2) + pair
+            butterfly(index)
+            filter_pair(jnp.minimum(index + 1, B * A // 2 - 1))
+            return carry
+
+        return lax.fori_loop(0, A // 2, pair_step, carry)
+
+    lax.fori_loop(0, B, col_step, 0)
+
+    def transform_step(col, carry):
+        for pair in range(A // 2):
             spec = lax.dot_general(
-                dft_ref[...], zed[...], (((1,), (1,)), ((), ())), preferred_element_type=F32
+                dft_ref[...], zed[col * (A // 2) + pair], (((1,), (1,)), ((), ())), preferred_element_type=F32
             )
             for which in range(2):
                 turn[pl.ds(2 * pair + which, 512, stride=A), :] = spec[:, which * LANES:(which + 1) * LANES]
-            return carry
-
-        lax.fori_loop(0, A // 2, pair_step, 0)
         out_ref[:, col] = turn[...].reshape(128, 2, 16, LANES).astype(BF16)
         return carry
 
-    lax.fori_loop(0, B, col_step, 0)
+    lax.fori_loop(0, B, transform_step, 0)
 
 
 def in_hbm(x):
@@ -183,7 +188,7 @@
             pltpu.VMEM((8, 256), F32),
             pltpu.VMEM((TAPS * 16, LANES), F32),
             pltpu.VMEM((2, 2, FRAMES * 16, LANES), F32),
-            pltpu.VMEM((256, 512), BF16),
+            pltpu.VMEM((B * A // 2, 256, 512), BF16),
             pltpu.VMEM((512 * A, LANES), F32),
             pltpu.SemaphoreType.DMA((B + 3,)),
         ],
@@ -202,7 +207,7 @@
                 turn[h, pl.ds(high * 1024 + low, 128, stride=8), :] = got[:, h * LANES:(h + 1) * LANES]
         return carry
 
-    lax.fori_loop(0, NCOL // 8, row_step, 0)
+    lax.fori_loop(0, NCOL // 8, row_step, 0, unroll=2)
 
     def col_step(g, carry):
         pows = []
@@ -222,7 +227,7 @@
         )
         return carry
 
-    lax.fori_loop(0, COLS, col_step, 0)
+    lax.fori_loop(0, COLS, col_step, 0, unroll=4)
 
 
 def beamform(got):

time: 103 us -> 96.9 us (0.941)
  Pallas kernels: 25.8 us -> 20.1 us
    pallas_call x1, Pallas kernels: 15.8 us -> 12.5 us  [channelize(): pl.pallas_call(channelize_kernel, name='channelize', in_specs=[pl.BlockSp...]
    pallas_call x1, Pallas kernels: 8.26 us -> 5.76 us  [beamform(): pl.pallas_call(beam_kernel, name='beamform', out_shape=jax.ShapeDtypeStru...]
where the time goes in v2:
time: 96.9 us; the launch traced here: 96.7 us
  blocking collectives  76.6 us (79%)
  Pallas kernels  20.1 us (21%)
    all_to_all x1, blocking collectives, body(): gathered = lax.all_to_all(spectra, ('row', 'col'), 0, 0, tiled=True)  63.7 us
    all_to_all x1, blocking collectives, body(): swapped = lax.all_to_all(partial, 'col', 0, 0, tiled=True)  12.9 us
    pallas_call x1, Pallas kernels, channelize(): pl.pallas_call(channelize_kernel, name='channelize', in_specs=[pl.BlockSp...  12.5 us
    pallas_call x1, Pallas kernels, beamform(): pl.pallas_call(beam_kernel, name='beamform', out_shape=jax.ShapeDtypeStru...  5.76 us

profile of v2, /device:TPU:1, one launch (start us, length us, event | category | flops | bytes accessed | tf_op | source)
XLA Modules:
  0.0 96.7 jit_solution(2971092039855906072)
XLA Ops:
  0.0 12.5 %channelize.1 = bf16[128,4,2,16,128]{4,3,2,1,0:T(8,128)(2,1)S(1)} custom-call(bf16[2,8,4,496,128]{4,3,2,1,0:T(8,128)(2,1)} %bitcast.8, f32[16,1024]{1,0:T(8,128)} %fir_hbm.1, bf16[512,512]{1,0:T(8,128)(2,1)} %constant.10.clone.dft_hbm, f32[8,256]{1,0:T(8,128)} %constant.11.clone.tw_hbm), custom_call_target="tpu_custom_call" | custom-call | tf_op jit(solution)/shard_map/channelize/pallas_call | solution.py:179
  12.5 0.0 copy-start
  12.5 0.0 copy-start.1
  12.5 0.0 copy-start.2
  12.6 63.7 %all_to_all.10 = bf16[128,4,2,16,128]{4,3,2,1,0:T(8,128)(2,1)S(1)} all-to-all(bf16[128,4,2,16,128]{4,3,2,1,0:T(8,128)(2,1)S(1)} %channelize.1), channel_id=1, replica_groups=mesh['row'=8,'col'=16] {'row','col'}, dimensions={0} | all-to-all | bytes 8388608 | tf_op jit(solution)/shard_map/all_to_all | solution.py:264
  76.2 0.0 copy-done
  76.2 0.0 copy-done.1
  76.2 0.0 copy-done.2
  76.2 5.8 %beamform.1 = f32[16,16,256]{2,1,0:T(8,128)S(1)} custom-call(bf16[8,16,4,2,16,128]{5,4,3,2,1,0:T(8,128)(2,1)S(1)} %bitcast.7, bf16[128,128]{1,0:T(8,128)(2,1)S(1)} %copy-done.1, bf16[128,128]{1,0:T(8,128)(2,1)S(1)} %copy-done, bf16[16,256]{1,0:T(8,128)(2,1)S(1)} %copy-done.2), custom_call_target="tpu_custom_call" | custom-call | tf_op jit(solution)/shard_map/beamform/pallas_call | solution.py:234
  82.0 12.9 %all_to_all.11.in_ref = f32[16,16,256]{2,1,0:T(8,128)} all-to-all(f32[16,16,256]{2,1,0:T(8,128)S(1)} %beamform.1), channel_id=1, replica_groups=mesh['row'=8,'col'=16] {'col'}, dimensions={0} | all-to-all | bytes 524288 | tf_op jit(solution)/shard_map/all_to_all | solution.py:266
  94.9 1.8 %finish.1 = f32[512,128]{1,0:T(8,128)} custom-call(f32[16,16,256]{2,1,0:T(8,128)} %all_to_all.11.in_ref), custom_call_target="tpu_custom_call" | custom-call | tf_op jit(solution)/shard_map/finish/pallas_call | solution.py:255
Async XLA Ops:
  12.5 63.7 %copy-start = (bf16[128,128]{1,0:T(8,128)(2,1)S(1)}, bf16[128,128]{1,0:T(8,128)(2,1)}, u32[]{:S(2)}) copy-start(bf16[128,128]{1,0:T(8,128)(2,1)} %constant.13.clone.col_ref) | copy-start | bytes 98308
  12.5 63.7 %copy-start.1 = (bf16[128,128]{1,0:T(8,128)(2,1)S(1)}, bf16[128,128]{1,0:T(8,128)(2,1)}, u32[]{:S(2)}) copy-start(bf16[128,128]{1,0:T(8,128)(2,1)} %constant.12.clone.row_ref) | copy-start | bytes 98308
  12.5 63.7 %copy-start.2 = (bf16[16,256]{1,0:T(8,128)(2,1)S(1)}, bf16[16,256]{1,0:T(8,128)(2,1)}, u32[]{:S(2)}) copy-start(bf16[16,256]{1,0:T(8,128)(2,1)} %constant.14.clone.sum_ref) | copy-start | bytes 24580

commit v3 on v2

--- a/solution.py
+++ b/solution.py
@@ -72,16 +72,19 @@
 
 
 def channelize_kernel(x_hbm, fir_hbm, dft_hbm, tw_hbm, out_ref, x_ref, fir_ref, dft_ref, tw_ref, coef, filt, zed, turn, sems):
-    x_copies = [pltpu.make_async_copy(x_hbm.at[:, :, b], x_ref.at[b], sems.at[b]) for b in range(B)]
+    x_copies = [pltpu.make_async_copy(x_hbm.at[:, :, b], x_ref.at[b], sems.at[b]) for b in range(1, B)]
+    head_copy = pltpu.make_async_copy(x_hbm.at[:, :2, 0], x_ref.at[0, :, :2], sems.at[0])
+    tail_copy = pltpu.make_async_copy(x_hbm.at[:, 2:, 0], x_ref.at[0, :, 2:], sems.at[B + 3])
     fir_copy = pltpu.make_async_copy(fir_hbm, fir_ref, sems.at[B])
     dft_copy = pltpu.make_async_copy(dft_hbm, dft_ref, sems.at[B + 1])
     tw_copy = pltpu.make_async_copy(tw_hbm, tw_ref, sems.at[B + 2])
     fir_copy.start()
-    x_copies[0].start()
+    head_copy.start()
+    tail_copy.start()
     tw_copy.start()
+    for copy in x_copies:
+        copy.start()
     dft_copy.start()
-    for b in range(1, B):
-        x_copies[b].start()
     fir_copy.wait()
     for s in range(8):
         piece = fir_ref[:, s * LANES:(s + 1) * LANES]
@@ -136,25 +139,25 @@
                         zed[slot, r0:r0 + 16, lo * LANES:(lo + 1) * LANES] = zr.astype(BF16)
                         zed[slot, r0:r0 + 16, (2 + lo) * LANES:(3 + lo) * LANES] = zi.astype(BF16)
 
-    x_copies[0].wait()
+    head_copy.wait()
     filter_pair(0)
     tw_copy.wait()
+    tail_copy.wait()
+
+    def pair_step(index, carry):
+        col = (index + 1) // (A // 2)
+
+        @pl.when(index % (A // 2) == A // 2 - 1)
+        def _():
+            pltpu.make_async_copy(x_hbm.at[:, :, col], x_ref.at[col], sems.at[col]).wait()
+
+        butterfly(index)
+        filter_pair(index + 1)
+        return carry
+
+    lax.fori_loop(0, B * A // 2 - 1, pair_step, 0)
+    butterfly(B * A // 2 - 1)
     dft_copy.wait()
-
-    def col_step(col, carry):
-        @pl.when(col < B - 1)
-        def _():
-            pltpu.make_async_copy(x_hbm.at[:, :, col + 1], x_ref.at[col + 1], sems.at[col + 1]).wait()
-
-        def pair_step(pair, carry):
-            index = col * (A // 2) + pair
-            butterfly(index)
-            filter_pair(jnp.minimum(index + 1, B * A // 2 - 1))
-            return carry
-
-        return lax.fori_loop(0, A // 2, pair_step, carry)
-
-    lax.fori_loop(0, B, col_step, 0)
 
     def transform_step(col, carry):
         for pair in range(A // 2):
@@ -190,7 +193,7 @@
             pltpu.VMEM((2, 2, FRAMES * 16, LANES), F32),
             pltpu.VMEM((B * A // 2, 256, 512), BF16),
             pltpu.VMEM((512 * A, LANES), F32),
-            pltpu.SemaphoreType.DMA((B + 3,)),
+            pltpu.SemaphoreType.DMA((B + 4,)),
         ],
         compiler_params=pltpu.CompilerParams(vmem_limit_bytes=40 << 20),
     )(in_hbm(flat), in_hbm(fir), in_hbm(jnp.asarray(dft_table())), in_hbm(jnp.asarray(twiddle_table())))
@@ -207,7 +210,7 @@
                 turn[h, pl.ds(high * 1024 + low, 128, stride=8), :] = got[:, h * LANES:(h + 1) * LANES]
         return carry
 
-    lax.fori_loop(0, NCOL // 8, row_step, 0, unroll=2)
+    lax.fori_loop(0, NCOL // 8, row_step, 0, unroll=8)
 
     def col_step(g, carry):
         pows = []
@@ -227,7 +230,7 @@
         )
         return carry
 
-    lax.fori_loop(0, COLS, col_step, 0, unroll=4)
+    lax.fori_loop(0, COLS, col_step, 0, unroll=16)
 
 
 def beamform(got):
@@ -255,8 +258,9 @@
     return pl.pallas_call(
         finish_kernel,
         name="finish",
+        in_specs=[pl.BlockSpec(memory_space=pltpu.VMEM)],
         out_shape=jax.ShapeDtypeStruct((256 * POL, LANES), F32),
-    )(got)
+    )(pltpu.with_memory_space_constraint(got, pltpu.VMEM))
 
 
 def body(volts, fir):

time: 96.9 us -> 94.1 us (0.971)
  Pallas kernels: 20.1 us -> 17.3 us
    pallas_call x1, Pallas kernels: 12.5 us -> 11.5 us  [channelize(): pl.pallas_call(channelize_kernel, name='channelize', in_specs=[pl.BlockSp...]
where the time goes in v3:
time: 94.1 us; the launch traced here: 93.9 us
  blocking collectives  76.5 us (81%)
  Pallas kernels  17.3 us (18%)
    all_to_all x1, blocking collectives, body(): gathered = lax.all_to_all(spectra, ('row', 'col'), 0, 0, tiled=True)  63.7 us
    all_to_all x1, blocking collectives, body(): swapped = lax.all_to_all(partial, 'col', 0, 0, tiled=True)  12.8 us
    pallas_call x1, Pallas kernels, channelize(): pl.pallas_call(channelize_kernel, name='channelize', in_specs=[pl.BlockSp...  11.5 us
    pallas_call x1, Pallas kernels, beamform(): pl.pallas_call(beam_kernel, name='beamform', out_shape=jax.ShapeDtypeStru...  5.02 us

profile of v3, /device:TPU:1, one launch (start us, length us, event | category | flops | bytes accessed | tf_op | source)
XLA Modules:
  0.0 93.9 jit_solution(1986682302801209987)
XLA Ops:
  0.0 11.5 %channelize.1 = bf16[128,4,2,16,128]{4,3,2,1,0:T(8,128)(2,1)S(1)} custom-call(bf16[2,8,4,496,128]{4,3,2,1,0:T(8,128)(2,1)} %bitcast.8, f32[16,1024]{1,0:T(8,128)} %fir_hbm.1, bf16[512,512]{1,0:T(8,128)(2,1)} %constant.10.clone.dft_hbm, f32[8,256]{1,0:T(8,128)} %constant.11.clone.tw_hbm), custom_call_target="tpu_custom_call" | custom-call | tf_op jit(solution)/shard_map/channelize/pallas_call | solution.py:182
  11.5 0.0 copy-start
  11.5 0.0 copy-start.1
  11.5 0.0 copy-start.2
  11.5 63.7 %all_to_all.10 = bf16[128,4,2,16,128]{4,3,2,1,0:T(8,128)(2,1)S(1)} all-to-all(bf16[128,4,2,16,128]{4,3,2,1,0:T(8,128)(2,1)S(1)} %channelize.1), channel_id=1, replica_groups=mesh['row'=8,'col'=16] {'row','col'}, dimensions={0} | all-to-all | bytes 8388608 | tf_op jit(solution)/shard_map/all_to_all | solution.py:268
  75.2 0.0 copy-done
  75.2 0.0 copy-done.1
  75.2 0.0 copy-done.2
  75.2 5.0 %beamform.1 = f32[16,16,256]{2,1,0:T(8,128)S(1)} custom-call(bf16[8,16,4,2,16,128]{5,4,3,2,1,0:T(8,128)(2,1)S(1)} %bitcast.7, bf16[128,128]{1,0:T(8,128)(2,1)S(1)} %copy-done.1, bf16[128,128]{1,0:T(8,128)(2,1)S(1)} %copy-done, bf16[16,256]{1,0:T(8,128)(2,1)S(1)} %copy-done.2), custom_call_target="tpu_custom_call" | custom-call | tf_op jit(solution)/shard_map/beamform/pallas_call | solution.py:237
  80.2 12.8 %all_to_all.11.in_ref = f32[16,16,256]{2,1,0:T(8,128)S(1)} all-to-all(f32[16,16,256]{2,1,0:T(8,128)S(1)} %beamform.1), channel_id=1, replica_groups=mesh['row'=8,'col'=16] {'col'}, dimensions={0} | all-to-all | bytes 524288 | tf_op jit(solution)/shard_map/all_to_all | solution.py:270
  93.0 0.8 finish.1
Async XLA Ops:
  11.5 63.7 %copy-start = (bf16[128,128]{1,0:T(8,128)(2,1)S(1)}, bf16[128,128]{1,0:T(8,128)(2,1)}, u32[]{:S(2)}) copy-start(bf16[128,128]{1,0:T(8,128)(2,1)} %constant.13.clone.col_ref) | copy-start | bytes 98308
  11.5 63.7 %copy-start.1 = (bf16[128,128]{1,0:T(8,128)(2,1)S(1)}, bf16[128,128]{1,0:T(8,128)(2,1)}, u32[]{:S(2)}) copy-start(bf16[128,128]{1,0:T(8,128)(2,1)} %constant.12.clone.row_ref) | copy-start | bytes 98308
  11.5 63.7 %copy-start.2 = (bf16[16,256]{1,0:T(8,128)(2,1)S(1)}, bf16[16,256]{1,0:T(8,128)(2,1)}, u32[]{:S(2)}) copy-start(bf16[16,256]{1,0:T(8,128)(2,1)} %constant.14.clone.sum_ref) | copy-start | bytes 24580

commit v4 on v3

--- a/solution.py
+++ b/solution.py
@@ -1,4 +1,6 @@
 import functools
+
+import math
 
 import jax
 import jax.numpy as jnp
@@ -39,14 +41,13 @@
 
 
 def dft_table():
-    k = np.arange(256)
-    table = complex_table(2.0 * np.pi * (np.outer(k, k) % 256) / 256)
-    return table.transpose(0, 1, 3, 2).reshape(512, 512)
+    k = np.arange(LANES)
+    table = complex_table(2.0 * np.pi * (np.outer(k, k) % LANES) / LANES)
+    return table.transpose(0, 1, 3, 2).reshape(2 * LANES, 2 * LANES)
 
 
 def twiddle_table():
-    n = np.arange(256)
-    angle = 2.0 * np.pi * np.outer(np.arange(4), n) / NCHAN
+    angle = 2.0 * np.pi * np.outer(np.arange(8), np.arange(LANES)) / NCHAN
     return np.concatenate([np.cos(angle), np.sin(angle)]).astype(np.float32)
 
 
@@ -56,18 +57,19 @@
 
 
 def row_matrix():
-    table = spatial(NROW).reshape(NROW, 2, ROWS, A, 2)
-    return table.transpose(0, 1, 2, 4, 3).reshape(2 * NROW, 2 * NROW)
+    table = spatial(NROW).reshape(NROW, 2, ROWS, A // 4, 4, 2)
+    return table.transpose(0, 1, 2, 3, 5, 4).reshape(2 * NROW, 2 * NROW)
 
 
 def col_matrix():
-    table = spatial(NCOL).reshape(NCOL, 2, 8, 8, 2)
+    table = spatial(NCOL).reshape(NCOL, 2, COLS, B, 2)
     return table.transpose(1, 0, 2, 4, 3).reshape(2 * NCOL, 2 * NCOL)
 
 
 def sum_matrix():
     eye = np.eye(8, dtype=np.float32).reshape(2, 4, 2, 4)
-    full = np.einsum("hqHQ,pP,f->phqHQPf", eye, np.eye(2, dtype=np.float32), np.ones(FRAMES, np.float32))
+    ones = np.ones(4, np.float32)
+    full = np.einsum("hqHQ,pP,g,f->phqHQgPf", eye, np.eye(2, dtype=np.float32), ones, ones)
     return (full.reshape(16, 256) / (FRAMES * NROW * NCOL)).astype(jnp.bfloat16)
 
 
@@ -104,40 +106,54 @@
                     terms = [t.astype(F32) for t in terms]
                     while len(terms) > 1:
                         terms = [a + b for a, b in zip(terms[::2], terms[1::2])]
-                    row = (f // 8) * 128 + f % 8
-                    filt[which, part, pl.ds(row, 16, stride=8), :] = terms[0]
-
-    def load_rows(which, part, row):
-        lo = filt[which, part, row * 8:row * 8 + 8, :]
-        hi = filt[which, part, 128 + row * 8:128 + row * 8 + 8, :]
+                    row = (f // 4) * 64 + f % 4
+                    filt[which, part, pl.ds(row, 16, stride=4), :] = terms[0]
+
+    def load_rows(which, part, t, j):
+        lo = filt[which, part, 128 * t + 8 * j:128 * t + 8 * j + 8, :]
+        hi = filt[which, part, 128 * t + 64 + 8 * j:128 * t + 64 + 8 * j + 8, :]
         return jnp.concatenate([lo, hi], axis=0)
 
+    def dft4(y):
+        (r0, i0), (r1, i1), (r2, i2), (r3, i3) = y
+        sr0, si0 = r0 + r2, i0 + i2
+        sr1, si1 = r1 + r3, i1 + i3
+        dr0, di0 = r0 - r2, i0 - i2
+        dr1, di1 = r1 - r3, i1 - i3
+        return [
+            (sr0 + sr1, si0 + si1),
+            (dr0 + di1, di0 - dr1),
+            (sr0 - sr1, si0 - si1),
+            (dr0 - di1, di0 + dr1),
+        ]
+
     def butterfly(slot):
+        half = math.sqrt(0.5)
         for which in range(2):
-            for p in range(POL):
-                for lo in range(2):
-                    rows = [2 * (2 * j + lo) + p for j in range(4)]
-                    re = [load_rows(which, 0, row) for row in rows]
-                    im = [load_rows(which, 1, row) for row in rows]
-                    sr0, si0 = re[0] + re[2], im[0] + im[2]
-                    sr1, si1 = re[1] + re[3], im[1] + im[3]
-                    dr0, di0 = re[0] - re[2], im[0] - im[2]
-                    dr1, di1 = re[1] - re[3], im[1] - im[3]
-                    outs = [
-                        (sr0 + sr1, si0 + si1),
-                        (dr0 + di1, di0 - dr1),
-                        (sr0 - sr1, si0 - si1),
-                        (dr0 - di1, di0 + dr1),
-                    ]
-                    for q in range(4):
-                        zr, zi = outs[q]
+            for t in range(2):
+                re = [load_rows(which, 0, t, j) for j in range(8)]
+                im = [load_rows(which, 1, t, j) for j in range(8)]
+                sums = [(re[j] + re[j + 4], im[j] + im[j + 4]) for j in range(4)]
+                (r0, i0), (r1, i1), (r2, i2), (r3, i3) = [
+                    (re[j] - re[j + 4], im[j] - im[j + 4]) for j in range(4)
+                ]
+                odds = [
+                    (r0, i0),
+                    ((r1 + i1) * half, (i1 - r1) * half),
+                    (i2, -r2),
+                    ((i3 - r3) * half, (r3 + i3) * -half),
+                ]
+                for parity, outs in enumerate((dft4(sums), dft4(odds))):
+                    for r in range(4):
+                        q = 2 * r + parity
+                        zr, zi = outs[r]
                         if q > 0:
-                            cosine = tw_ref[q:q + 1, lo * LANES:(lo + 1) * LANES]
-                            sine = tw_ref[4 + q:5 + q, lo * LANES:(lo + 1) * LANES]
+                            cosine = tw_ref[q:q + 1, :]
+                            sine = tw_ref[8 + q:9 + q, :]
                             zr, zi = zr * cosine + zi * sine, zi * cosine - zr * sine
-                        r0 = which * LANES + q * 32 + p * 16
-                        zed[slot, r0:r0 + 16, lo * LANES:(lo + 1) * LANES] = zr.astype(BF16)
-                        zed[slot, r0:r0 + 16, (2 + lo) * LANES:(3 + lo) * LANES] = zi.astype(BF16)
+                        row = q * 32 + t * 16
+                        zed[2 * slot + which, row:row + 16, :LANES] = zr.astype(BF16)
+                        zed[2 * slot + which, row:row + 16, LANES:] = zi.astype(BF16)
 
     head_copy.wait()
     filter_pair(0)
@@ -160,16 +176,20 @@
     dft_copy.wait()
 
     def transform_step(col, carry):
-        for pair in range(A // 2):
+        for ant in range(A):
             spec = lax.dot_general(
-                dft_ref[...], zed[col * (A // 2) + pair], (((1,), (1,)), ((), ())), preferred_element_type=F32
+                dft_ref[...], zed[col * A + ant], (((1,), (1,)), ((), ())), preferred_element_type=F32
             )
-            for which in range(2):
-                turn[pl.ds(2 * pair + which, 512, stride=A), :] = spec[:, which * LANES:(which + 1) * LANES]
-        out_ref[:, col] = turn[...].reshape(128, 2, 16, LANES).astype(BF16)
-        return carry
-
-    lax.fori_loop(0, B, transform_step, 0)
+            for h in range(2):
+                row = (2 * h + ant // 4) * 1024 + ant % 4
+                turn[col % 2, pl.ds(row, 256, stride=4), :] = spec[:, h * LANES:(h + 1) * LANES]
+        for h in range(2):
+            rows = [turn[col % 2, i * 1024:(i + 1) * 1024, :].reshape(128, 8, LANES) for i in (2 * h, 2 * h + 1)]
+            out_ref[:, col, h] = jnp.concatenate(rows, axis=1).astype(BF16)
+        return carry
+
+    for col in range(B):
+        transform_step(col, 0)
 
 
 def in_hbm(x):
@@ -187,12 +207,12 @@
         scratch_shapes=[
             pltpu.VMEM((B, 2, A, BLOCKS * 16, LANES), BF16),
             pltpu.VMEM((TAPS, NCHAN), F32),
-            pltpu.VMEM((512, 512), BF16),
-            pltpu.VMEM((8, 256), F32),
+            pltpu.VMEM((256, 256), BF16),
+            pltpu.VMEM((16, LANES), F32),
             pltpu.VMEM((TAPS * 16, LANES), F32),
             pltpu.VMEM((2, 2, FRAMES * 16, LANES), F32),
-            pltpu.VMEM((B * A // 2, 256, 512), BF16),
-            pltpu.VMEM((512 * A, LANES), F32),
+            pltpu.VMEM((B * A, 256, 256), BF16),
+            pltpu.VMEM((2, 512 * A, LANES), F32),
             pltpu.SemaphoreType.DMA((B + 4,)),
         ],
         compiler_params=pltpu.CompilerParams(vmem_limit_bytes=40 << 20),
@@ -207,7 +227,7 @@
             )
             got = jnp.dot(row_ref[...], piece, preferred_element_type=F32)
             for h in range(2):
-                turn[h, pl.ds(high * 1024 + low, 128, stride=8), :] = got[:, h * LANES:(h + 1) * LANES]
+                turn[h, pl.ds((2 * high + low // B) * 512 + low % B, 128, stride=4), :] = got[:, h * LANES:(h + 1) * LANES]
         return carry
 
     lax.fori_loop(0, NCOL // 8, row_step, 0, unroll=8)
@@ -215,10 +235,10 @@
     def col_step(g, carry):
         pows = []
         for j in range(4):
-            base = (4 * g + j) * 16
+            base = (4 * g + j) * 8
             mids = []
             for h in range(2):
-                rows = [turn[h, pl.ds(pl.multiple_of(high * 1024 + base, 16), 16), :] for high in range(8)]
+                rows = [turn[h, pl.ds(pl.multiple_of(c * 512 + base, 8), 8), :] for c in range(COLS)]
                 mids.append(jnp.concatenate(rows, axis=0).astype(BF16))
             beam = jnp.dot(col_ref[...], jnp.concatenate(mids, axis=1), preferred_element_type=F32)
             re = beam[:NCOL]

time: 94.1 us -> 92 us (0.978)
  Pallas kernels: 17.3 us -> 15.3 us
    pallas_call x1, Pallas kernels: 11.5 us -> 9.85 us  [channelize(): pl.pallas_call(channelize_kernel, name='channelize', in_specs=[pl.BlockSp...]
where the time goes in v4:
time: 92 us; the launch traced here: 91.8 us
  blocking collectives  76.4 us (83%)
  Pallas kernels  15.3 us (17%)
    all_to_all x1, blocking collectives, body(): gathered = lax.all_to_all(spectra, ('row', 'col'), 0, 0, tiled=True)  63.7 us
    all_to_all x1, blocking collectives, body(): swapped = lax.all_to_all(partial, 'col', 0, 0, tiled=True)  12.8 us
    pallas_call x1, Pallas kernels, channelize(): pl.pallas_call(channelize_kernel, name='channelize', in_specs=[pl.BlockSp...  9.85 us
    pallas_call x1, Pallas kernels, beamform(): pl.pallas_call(beam_kernel, name='beamform', out_shape=jax.ShapeDtypeStru...  4.6 us

profile of v4, /device:TPU:1, one launch (start us, length us, event | category | flops | bytes accessed | tf_op | source)
XLA Modules:
  0.0 91.8 jit_solution(277572014441993139)
XLA Ops:
  0.0 9.9 %channelize.1 = bf16[128,4,2,16,128]{4,3,2,1,0:T(8,128)(2,1)S(1)} custom-call(bf16[2,8,4,496,128]{4,3,2,1,0:T(8,128)(2,1)} %bitcast.8, f32[16,1024]{1,0:T(8,128)} %fir_hbm.1, bf16[256,256]{1,0:T(8,128)(2,1)} %constant.10.clone.dft_hbm, f32[16,128]{1,0:T(8,128)} %constant.11.clone.tw_hbm), custom_call_target="tpu_custom_call" | custom-call | tf_op jit(solution)/shard_map/channelize/pallas_call | solution.py:202
  9.9 0.0 copy-start
  9.9 0.0 copy-start.1
  9.9 0.0 copy-start.2
  9.9 63.7 %all_to_all.10 = bf16[128,4,2,16,128]{4,3,2,1,0:T(8,128)(2,1)S(1)} all-to-all(bf16[128,4,2,16,128]{4,3,2,1,0:T(8,128)(2,1)S(1)} %channelize.1), channel_id=1, replica_groups=mesh['row'=8,'col'=16] {'row','col'}, dimensions={0} | all-to-all | bytes 8388608 | tf_op jit(solution)/shard_map/all_to_all | solution.py:288
  73.5 0.0 copy-done
  73.6 0.0 copy-done.1
  73.6 0.0 copy-done.2
  73.6 4.6 %beamform.1 = f32[16,16,256]{2,1,0:T(8,128)S(1)} custom-call(bf16[8,16,4,2,16,128]{5,4,3,2,1,0:T(8,128)(2,1)S(1)} %bitcast.7, bf16[128,128]{1,0:T(8,128)(2,1)S(1)} %copy-done.1, bf16[128,128]{1,0:T(8,128)(2,1)S(1)} %copy-done, bf16[16,256]{1,0:T(8,128)(2,1)S(1)} %copy-done.2), custom_call_target="tpu_custom_call" | custom-call | tf_op jit(solution)/shard_map/beamform/pallas_call | solution.py:257
  78.2 12.8 %all_to_all.11.in_ref = f32[16,16,256]{2,1,0:T(8,128)S(1)} all-to-all(f32[16,16,256]{2,1,0:T(8,128)S(1)} %beamform.1), channel_id=1, replica_groups=mesh['row'=8,'col'=16] {'col'}, dimensions={0} | all-to-all | bytes 524288 | tf_op jit(solution)/shard_map/all_to_all | solution.py:290
  90.9 0.8 finish.1
Async XLA Ops:
  9.9 63.7 %copy-start = (bf16[128,128]{1,0:T(8,128)(2,1)S(1)}, bf16[128,128]{1,0:T(8,128)(2,1)}, u32[]{:S(2)}) copy-start(bf16[128,128]{1,0:T(8,128)(2,1)} %constant.13.clone.col_ref) | copy-start | bytes 98308
  9.9 63.7 %copy-start.1 = (bf16[128,128]{1,0:T(8,128)(2,1)S(1)}, bf16[128,128]{1,0:T(8,128)(2,1)}, u32[]{:S(2)}) copy-start(bf16[128,128]{1,0:T(8,128)(2,1)} %constant.12.clone.row_ref) | copy-start | bytes 98308
  9.9 63.7 %copy-start.2 = (bf16[16,256]{1,0:T(8,128)(2,1)S(1)}, bf16[16,256]{1,0:T(8,128)(2,1)}, u32[]{:S(2)}) copy-start(bf16[16,256]{1,0:T(8,128)(2,1)} %constant.14.clone.sum_ref) | copy-start | bytes 24580

commit v5 on v4

--- a/solution.py
+++ b/solution.py
@@ -73,7 +73,7 @@
     return (full.reshape(16, 256) / (FRAMES * NROW * NCOL)).astype(jnp.bfloat16)
 
 
-def channelize_kernel(x_hbm, fir_hbm, dft_hbm, tw_hbm, out_ref, x_ref, fir_ref, dft_ref, tw_ref, coef, filt, zed, turn, sems):
+def channelize_kernel(x_hbm, fir_hbm, dft_hbm, tw_hbm, out_ref, x_ref, fir_ref, dft_ref, tw_ref, coef, coef16, filt, zed, turn, sems):
     x_copies = [pltpu.make_async_copy(x_hbm.at[:, :, b], x_ref.at[b], sems.at[b]) for b in range(1, B)]
     head_copy = pltpu.make_async_copy(x_hbm.at[:, :2, 0], x_ref.at[0, :, :2], sems.at[0])
     tail_copy = pltpu.make_async_copy(x_hbm.at[:, 2:, 0], x_ref.at[0, :, 2:], sems.at[B + 3])
@@ -92,12 +92,13 @@
         piece = fir_ref[:, s * LANES:(s + 1) * LANES]
         for p in range(POL):
             coef[pl.ds(2 * s + p, TAPS, stride=16), :] = piece
+    coef16[...] = coef[...].astype(BF16)
 
     def filter_pair(index, units=((0, 0), (0, 1), (1, 0), (1, 1))):
         col = index // (A // 2)
         pair = index % (A // 2)
         for which, part in units:
-                taps = [coef[16 * t:16 * t + 16, :].astype(BF16) for t in range(TAPS)]
+                taps = [coef16[16 * t:16 * t + 16, :] for t in range(TAPS)]
                 xs = [x_ref[col, part, 2 * pair + which, 16 * i:16 * i + 16, :] for i in range(BLOCKS)]
                 for f in range(FRAMES):
                     terms = [taps[t] * xs[f + t] for t in range(TAPS)]
@@ -210,6 +211,7 @@
             pltpu.VMEM((256, 256), BF16),
             pltpu.VMEM((16, LANES), F32),
             pltpu.VMEM((TAPS * 16, LANES), F32),
+            pltpu.VMEM((TAPS * 16, LANES), BF16),
             pltpu.VMEM((2, 2, FRAMES * 16, LANES), F32),
             pltpu.VMEM((B * A, 256, 256), BF16),
             pltpu.VMEM((2, 512 * A, LANES), F32),
@@ -247,7 +249,7 @@
         power = jnp.concatenate(pows, axis=0)
         out_ref[g] = lax.dot_general(
             sum_ref[...], power, (((1,), (1,)), ((), ())), preferred_element_type=F32
-        )
+        ).astype(BF16)
         return carry
 
     lax.fori_loop(0, COLS, col_step, 0, unroll=16)
@@ -257,7 +259,7 @@
     return pl.pallas_call(
         beam_kernel,
         name="beamform",
-        out_shape=jax.ShapeDtypeStruct((COLS, 16, 256), F32),
+        out_shape=jax.ShapeDtypeStruct((COLS, 16, 256), BF16),
         scratch_shapes=[pltpu.VMEM((2, 128 * NCOL, LANES), F32)],
         compiler_params=pltpu.CompilerParams(vmem_limit_bytes=40 << 20),
     )(
@@ -269,8 +271,9 @@
 
 
 def finish_kernel(in_ref, out_ref):
+    wide = in_ref[...].astype(F32)
     for p in range(POL):
-        piece = in_ref[:, p * 8:(p + 1) * 8, :].reshape(128, 256)
+        piece = wide[:, p * 8:(p + 1) * 8, :].reshape(128, 256)
         out_ref[pl.ds(p, 256, stride=2), :] = piece.T
 
 

time: 92 us -> 95.1 us (1.034)
  Pallas kernels: 15.3 us -> 19.6 us
  blocking collectives: 76.4 us -> 75.2 us
    pallas_call x1, Pallas kernels: 9.85 us -> 14.2 us  [channelize(): pl.pallas_call(channelize_kernel, name='channelize', in_specs=[pl.BlockSp...]
    all_to_all x1, blocking collectives: 12.8 us -> 11.6 us  [body(): swapped = lax.all_to_all(partial, 'col', 0, 0, tiled=True)]
where the time goes in v5:
time: 95.1 us; the launch traced here: 94.9 us
  blocking collectives  75.2 us (79%)
  Pallas kernels  19.6 us (21%)
    all_to_all x1, blocking collectives, body(): gathered = lax.all_to_all(spectra, ('row', 'col'), 0, 0, tiled=True)  63.7 us
    pallas_call x1, Pallas kernels, channelize(): pl.pallas_call(channelize_kernel, name='channelize', in_specs=[pl.BlockSp...  14.2 us
    all_to_all x1, blocking collectives, body(): swapped = lax.all_to_all(partial, 'col', 0, 0, tiled=True)  11.6 us
    pallas_call x1, Pallas kernels, beamform(): pl.pallas_call(beam_kernel, name='beamform', out_shape=jax.ShapeDtypeStru...  4.6 us

profile of v5, /device:TPU:1, one launch (start us, length us, event | category | flops | bytes accessed | tf_op | source)
XLA Modules:
  0.0 94.9 jit_solution(6283446627436727029)
XLA Ops:
  0.0 14.2 %channelize.1 = bf16[128,4,2,16,128]{4,3,2,1,0:T(8,128)(2,1)S(1)} custom-call(bf16[2,8,4,496,128]{4,3,2,1,0:T(8,128)(2,1)} %bitcast.8, f32[16,1024]{1,0:T(8,128)} %fir_hbm.1, bf16[256,256]{1,0:T(8,128)(2,1)} %constant.10.clone.dft_hbm, f32[16,128]{1,0:T(8,128)} %constant.11.clone.tw_hbm), custom_call_target="tpu_custom_call" | custom-call | tf_op jit(solution)/shard_map/channelize/pallas_call | solution.py:203
  14.2 0.0 copy-start
  14.2 0.0 copy-start.1
  14.3 0.0 copy-start.2
  14.3 63.7 %all_to_all.10 = bf16[128,4,2,16,128]{4,3,2,1,0:T(8,128)(2,1)S(1)} all-to-all(bf16[128,4,2,16,128]{4,3,2,1,0:T(8,128)(2,1)S(1)} %channelize.1), channel_id=1, replica_groups=mesh['row'=8,'col'=16] {'row','col'}, dimensions={0} | all-to-all | bytes 8388608 | tf_op jit(solution)/shard_map/all_to_all | solution.py:291
  77.9 0.0 copy-done
  77.9 0.0 copy-done.1
  77.9 0.0 copy-done.2
  77.9 4.6 %beamform.1 = bf16[16,16,256]{2,1,0:T(8,128)(2,1)S(1)} custom-call(bf16[8,16,4,2,16,128]{5,4,3,2,1,0:T(8,128)(2,1)S(1)} %bitcast.7, bf16[128,128]{1,0:T(8,128)(2,1)S(1)} %copy-done.1, bf16[128,128]{1,0:T(8,128)(2,1)S(1)} %copy-done, bf16[16,256]{1,0:T(8,128)(2,1)S(1)} %copy-done.2), custom_call_target="tpu_custom_call" | custom-call | tf_op jit(solution)/shard_map/beamform/pallas_call | solution.py:259
  82.5 11.6 %all_to_all.11.in_ref = bf16[16,16,256]{2,1,0:T(8,128)(2,1)S(1)} all-to-all(bf16[16,16,256]{2,1,0:T(8,128)(2,1)S(1)} %beamform.1), channel_id=1, replica_groups=mesh['row'=8,'col'=16] {'col'}, dimensions={0} | all-to-all | bytes 262144 | tf_op jit(solution)/shard_map/all_to_all | solution.py:293
  94.1 0.8 finish.1
Async XLA Ops:
  14.2 63.7 %copy-start = (bf16[128,128]{1,0:T(8,128)(2,1)S(1)}, bf16[128,128]{1,0:T(8,128)(2,1)}, u32[]{:S(2)}) copy-start(bf16[128,128]{1,0:T(8,128)(2,1)} %constant.13.clone.col_ref) | copy-start | bytes 98308
  14.2 63.7 %copy-start.1 = (bf16[128,128]{1,0:T(8,128)(2,1)S(1)}, bf16[128,128]{1,0:T(8,128)(2,1)}, u32[]{:S(2)}) copy-start(bf16[128,128]{1,0:T(8,128)(2,1)} %constant.12.clone.row_ref) | copy-start | bytes 98308
  14.3 63.7 %copy-start.2 = (bf16[16,256]{1,0:T(8,128)(2,1)S(1)}, bf16[16,256]{1,0:T(8,128)(2,1)}, u32[]{:S(2)}) copy-start(bf16[16,256]{1,0:T(8,128)(2,1)} %constant.14.clone.sum_ref) | copy-start | bytes 24580

commit v6 on v4

--- a/solution.py
+++ b/solution.py
@@ -219,7 +219,7 @@
     )(in_hbm(flat), in_hbm(fir), in_hbm(jnp.asarray(dft_table())), in_hbm(jnp.asarray(twiddle_table())))
 
 
-def beam_kernel(in_ref, row_ref, col_ref, sum_ref, out_ref, turn):
+def beam_kernel(in_ref, row_ref, col_ref, sum_ref, out_ref, turn, pows_ref):
     def row_step(high, carry):
         for low in range(8):
             piece = jnp.concatenate(
@@ -244,21 +244,23 @@
             re = beam[:NCOL]
             im = beam[NCOL:]
             pows.append((re * re + im * im).astype(BF16))
-        power = jnp.concatenate(pows, axis=0)
+        pows_ref[g] = jnp.concatenate(pows, axis=0)
+        return carry
+
+    lax.fori_loop(0, COLS, col_step, 0, unroll=16)
+
+    for g in range(COLS):
         out_ref[g] = lax.dot_general(
-            sum_ref[...], power, (((1,), (1,)), ((), ())), preferred_element_type=F32
-        )
-        return carry
-
-    lax.fori_loop(0, COLS, col_step, 0, unroll=16)
+            sum_ref[...], pows_ref[g], (((1,), (1,)), ((), ())), preferred_element_type=F32
+        ).astype(BF16)
 
 
 def beamform(got):
     return pl.pallas_call(
         beam_kernel,
         name="beamform",
-        out_shape=jax.ShapeDtypeStruct((COLS, 16, 256), F32),
-        scratch_shapes=[pltpu.VMEM((2, 128 * NCOL, LANES), F32)],
+        out_shape=jax.ShapeDtypeStruct((COLS, 16, 256), BF16),
+        scratch_shapes=[pltpu.VMEM((2, 128 * NCOL, LANES), F32), pltpu.VMEM((COLS, 256, 256), BF16)],
         compiler_params=pltpu.CompilerParams(vmem_limit_bytes=40 << 20),
     )(
         got.reshape(ROWS, COLS, B, 2, 16, LANES),
@@ -269,8 +271,9 @@
 
 
 def finish_kernel(in_ref, out_ref):
+    wide = in_ref[...].astype(F32)
     for p in range(POL):
-        piece = in_ref[:, p * 8:(p + 1) * 8, :].reshape(128, 256)
+        piece = wide[:, p * 8:(p + 1) * 8, :].reshape(128, 256)
         out_ref[pl.ds(p, 256, stride=2), :] = piece.T
 
 

time: 92 us -> 89.1 us (0.968)
  Pallas kernels: 15.3 us -> 13.6 us
  blocking collectives: 76.4 us -> 75.2 us
    pallas_call x1, Pallas kernels: 4.6 us -> 2.95 us  [beamform(): pl.pallas_call(beam_kernel, name='beamform', out_shape=jax.ShapeDtypeStru...]
    all_to_all x1, blocking collectives: 12.8 us -> 11.6 us  [body(): swapped = lax.all_to_all(partial, 'col', 0, 0, tiled=True)]
where the time goes in v6:
time: 89.1 us; the launch traced here: 88.9 us
  blocking collectives  75.2 us (84%)
  Pallas kernels  13.6 us (15%)
    all_to_all x1, blocking collectives, body(): gathered = lax.all_to_all(spectra, ('row', 'col'), 0, 0, tiled=True)  63.7 us
    all_to_all x1, blocking collectives, body(): swapped = lax.all_to_all(partial, 'col', 0, 0, tiled=True)  11.6 us
    pallas_call x1, Pallas kernels, channelize(): pl.pallas_call(channelize_kernel, name='channelize', in_specs=[pl.BlockSp...  9.85 us
    pallas_call x1, Pallas kernels, beamform(): pl.pallas_call(beam_kernel, name='beamform', out_shape=jax.ShapeDtypeStru...  2.95 us

profile of v6, /device:TPU:1, one launch (start us, length us, event | category | flops | bytes accessed | tf_op | source)
XLA Modules:
  0.0 88.9 jit_solution(1459504423672663335)
XLA Ops:
  0.0 9.9 %channelize.1 = bf16[128,4,2,16,128]{4,3,2,1,0:T(8,128)(2,1)S(1)} custom-call(bf16[2,8,4,496,128]{4,3,2,1,0:T(8,128)(2,1)} %bitcast.8, f32[16,1024]{1,0:T(8,128)} %fir_hbm.1, bf16[256,256]{1,0:T(8,128)(2,1)} %constant.10.clone.dft_hbm, f32[16,128]{1,0:T(8,128)} %constant.11.clone.tw_hbm), custom_call_target="tpu_custom_call" | custom-call | tf_op jit(solution)/shard_map/channelize/pallas_call | solution.py:202
  9.9 0.0 copy-start
  9.9 0.0 copy-start.1
  9.9 0.0 copy-start.2
  9.9 63.7 %all_to_all.10 = bf16[128,4,2,16,128]{4,3,2,1,0:T(8,128)(2,1)S(1)} all-to-all(bf16[128,4,2,16,128]{4,3,2,1,0:T(8,128)(2,1)S(1)} %channelize.1), channel_id=1, replica_groups=mesh['row'=8,'col'=16] {'row','col'}, dimensions={0} | all-to-all | bytes 8388608 | tf_op jit(solution)/shard_map/all_to_all | solution.py:291
  73.5 0.0 copy-done
  73.6 0.0 copy-done.1
  73.6 0.0 copy-done.2
  73.6 2.9 %beamform.1 = bf16[16,16,256]{2,1,0:T(8,128)(2,1)S(1)} custom-call(bf16[8,16,4,2,16,128]{5,4,3,2,1,0:T(8,128)(2,1)S(1)} %bitcast.7, bf16[128,128]{1,0:T(8,128)(2,1)S(1)} %copy-done.1, bf16[128,128]{1,0:T(8,128)(2,1)S(1)} %copy-done, bf16[16,256]{1,0:T(8,128)(2,1)S(1)} %copy-done.2), custom_call_target="tpu_custom_call" | custom-call | tf_op jit(solution)/shard_map/beamform/pallas_call | solution.py:259
  76.5 11.6 %all_to_all.11.in_ref = bf16[16,16,256]{2,1,0:T(8,128)(2,1)S(1)} all-to-all(bf16[16,16,256]{2,1,0:T(8,128)(2,1)S(1)} %beamform.1), channel_id=1, replica_groups=mesh['row'=8,'col'=16] {'col'}, dimensions={0} | all-to-all | bytes 262144 | tf_op jit(solution)/shard_map/all_to_all | solution.py:293
  88.1 0.8 finish.1
Async XLA Ops:
  9.9 63.7 %copy-start = (bf16[128,128]{1,0:T(8,128)(2,1)S(1)}, bf16[128,128]{1,0:T(8,128)(2,1)}, u32[]{:S(2)}) copy-start(bf16[128,128]{1,0:T(8,128)(2,1)} %constant.13.clone.col_ref) | copy-start | bytes 98308
  9.9 63.7 %copy-start.1 = (bf16[128,128]{1,0:T(8,128)(2,1)S(1)}, bf16[128,128]{1,0:T(8,128)(2,1)}, u32[]{:S(2)}) copy-start(bf16[128,128]{1,0:T(8,128)(2,1)} %constant.12.clone.row_ref) | copy-start | bytes 98308
  9.9 63.7 %copy-start.2 = (bf16[16,256]{1,0:T(8,128)(2,1)S(1)}, bf16[16,256]{1,0:T(8,128)(2,1)}, u32[]{:S(2)}) copy-start(bf16[16,256]{1,0:T(8,128)(2,1)} %constant.14.clone.sum_ref) | copy-start | bytes 24580
